TPU v7x, 32 devices: a whole 2x2x4 slice. The times are simulated.
32 devices in a mesh: event: 4 (over z), terrain: 8 (over y, x, core).
Axes of the slice: x: 2, y: 2, z: 4, core: 2. Of those that a mesh axis runs over, the one named last changes fastest.
Arguments:
- level_start: float32 [4, 256, 1024], P('event', 'terrain'), may hold values from -18 to 18
- bed_depth: float32 [256, 1024], P('terrain'), may hold values from 0.5 to 2
- wet_bits: int32 [4, 256, 1024], P('event', 'terrain'), may hold values from 0 to 255
- tile_owner: int32 [2048, 1], P('terrain'), may hold values from 0 to 7; in each aligned block of 256 rows (0 to 255, 256 to 511, ...) at most 48 rows name the same one
- vuln_weight: bfloat16 [128, 256], replicated, may hold values from -0.5 to 0.5
- vuln_bias: float32 [256], replicated, may hold values from -2 to 2
- account_index: int32 [3072, 128], P('terrain'), may hold values from 0 to 1023
- bin_index: int32 [3072, 128], P('terrain'), may hold values from 0 to 255
- exposure_value: bfloat16 [3072, 128], P('terrain'), may hold values from 1 to 10
- deductible: float32 [1024], replicated, may hold values from 0 to 0.8
- limit: float32 [1024], replicated, may hold values from 0.5 to 1.5
Outputs:
- level: float32 [4, 256, 1024], P('event', 'terrain')
- net_loss: bfloat16 [4, 1024, 256], P('event')
- portfolio: float32 [1024, 256], P('terrain')
Inputs may be any that keep to these rules, and one draw needn't show every extreme that they name: `tile_owner`: among the 256 tiles of one device no owner is named more than 48 times; in some devices one owner is named exactly 48 times. `wet_bits`: bit s (the value // 2**s, mod 2) is 1 where the cell is wet in substep s. `account_index`: rows of an owner's records that no tile reaches are not read.
All inputs are finite; a program needn't handle non-finite values.
Results may differ from a plain program's by a relative error of at most 0.0004.
The roundings to bfloat16 on the way count: a program that leaves them out, or rounds other values in their place, can miss the bound.
Values may be sent and summed in bfloat16 or wider, within the bound.
A program may use at most 64 MiB of HBM per device.

v0:
```python
import jax
import jax.numpy as jnp
from jax import lax
from jax.sharding import PartitionSpec as P

SUBSTEPS = 8


courant = 0.5
gravity = 1.0


def with_halo(cells, sides, width):
    for axis, dim in sides:
        count = lax.axis_size(axis)
        ends = count - 1
        head = lax.slice_in_dim(cells, 0, width, axis=dim)
        tail = lax.slice_in_dim(cells, cells.shape[dim] - width, cells.shape[dim], axis=dim)
        cells = jnp.concatenate(
            [
                lax.ppermute(tail, axis, [(i, (i + 1) % count) for i in range(ends)]),
                cells,
                lax.ppermute(head, axis, [((i + 1) % count, i) for i in range(ends)]),
            ],
            axis=dim,
        )
    return cells


def pad_columns(field):
    return jnp.pad(field[:, 1:-1, :], ((0, 0), (0, 0), (1, 1)))


def neighbour_mean(field):
    inner = pad_columns(field)
    return 0.25 * (field[:, 2:, :] + field[:, :-2, :] + inner[:, :, 2:] + inner[:, :, :-2])


def friedrichs_step(level, row_speed, col_speed, bed_depth, wet_factor):
    row_flow = bed_depth * row_speed
    col_flow = pad_columns(bed_depth * col_speed)
    level_pad = pad_columns(level)
    new_level = neighbour_mean(level) - 0.5 * courant * (
        row_flow[:, 2:, :] - row_flow[:, :-2, :] + (col_flow[:, :, 2:] - col_flow[:, :, :-2])
    )
    new_row = (
        neighbour_mean(row_speed) - 0.5 * courant * gravity * (level[:, 2:, :] - level[:, :-2, :])
    ) * wet_factor
    new_col = (
        neighbour_mean(col_speed)
        - 0.5 * courant * gravity * (level_pad[:, :, 2:] - level_pad[:, :, :-2])
    ) * wet_factor
    return (new_level, new_row, new_col)


def per_device(
    level_start,
    bed_depth,
    wet_bits,
    tile_owner,
    vuln_weight,
    vuln_bias,
    account_index,
    bin_index,
    exposure_value,
    deductible,
    limit,
):
    groups, rows, width = level_start.shape
    tile_cells, bin_count = vuln_weight.shape
    account_count = deductible.shape[0]
    owners = lax.axis_size("terrain")
    zeros = jnp.zeros_like(level_start)
    fields = jnp.stack([level_start, zeros, zeros, jnp.broadcast_to(bed_depth, level_start.shape)])
    widened = with_halo(fields, (("terrain", 2),), SUBSTEPS)
    wet_wide = with_halo(wet_bits, (("terrain", 1),), SUBSTEPS)
    level, row_speed, col_speed = (widened[0], widened[1], widened[2])
    bed_wide = widened[3][0]
    first_row = lax.axis_index("terrain") * rows - SUBSTEPS
    total_rows = rows * owners
    for step in range(SUBSTEPS):
        remain = SUBSTEPS - step - 1
        out_rows = rows + 2 * remain
        bed_now = bed_wide[step : step + out_rows + 2]
        row_ids = first_row + step + 1 + jnp.arange(out_rows, dtype=jnp.int32)
        inside = ((row_ids >= 0) & (row_ids < total_rows)).astype(jnp.float32)[None, :, None]
        wet_factor = (wet_wide[:, step + 1 : step + 1 + out_rows] // 2**step % 2).astype(
            jnp.float32
        ) * inside
        level, row_speed, col_speed = friedrichs_step(
            level, row_speed, col_speed, bed_now, wet_factor
        )
        level = level * inside
    pieces = level.astype(jnp.bfloat16).reshape(-1, tile_cells)
    slot_count = account_index.shape[0]
    capacity = slot_count // owners
    owner = tile_owner[:, 0]
    onehot = (owner[:, None] == jnp.arange(owners, dtype=jnp.int32)[None, :]).astype(jnp.int32)
    rank = jnp.sum((jnp.cumsum(onehot, axis=0) - onehot) * onehot, axis=1)
    place = owner * capacity + rank
    chosen = (place[:, None] == jnp.arange(slot_count, dtype=jnp.int32)[None, :]).astype(
        jnp.float32
    )
    marks_out = jnp.sum(chosen, axis=0).astype(jnp.bfloat16).reshape(owners, capacity)
    chosen = chosen.astype(jnp.bfloat16)
    pick = (((0,), (0,)), ((), ()))
    local_ratio = jax.nn.sigmoid(
        jnp.dot(pieces, vuln_weight, preferred_element_type=jnp.float32) + vuln_bias
    ).astype(jnp.bfloat16)
    outgoing = (
        lax.dot_general(chosen, local_ratio, pick, preferred_element_type=jnp.float32)
        .astype(jnp.bfloat16)
        .reshape(owners, capacity, bin_count)
    )
    ratio, marks = (
        lax.all_to_all(outgoing, "terrain", split_axis=0, concat_axis=0, tiled=True),
        lax.all_to_all(marks_out, "terrain", split_axis=0, concat_axis=0, tiled=True),
    )
    weighted = ratio.reshape(slot_count, bin_count) * marks.reshape(slot_count)[:, None]
    block = 32
    bin_range = jnp.arange(bin_count, dtype=jnp.int32)
    share_rows = account_count // owners
    lower = lax.axis_index("terrain") * share_rows
    scale = account_count / (rows * width * owners)
    columns = jnp.arange(account_count, dtype=jnp.int32)

    def add_block(total, block_id):
        first = block_id * block
        account_part = lax.dynamic_slice_in_dim(account_index, first, block, 0).reshape(-1)
        value_part = lax.dynamic_slice_in_dim(exposure_value, first, block, 0).reshape(-1)
        threshold_part = lax.dynamic_slice_in_dim(bin_index, first, block, 0)
        ratio_part = lax.dynamic_slice_in_dim(weighted, first, block, 0)
        left = jnp.where(
            account_part[:, None] == columns[None, :],
            value_part[:, None],
            jnp.zeros((), jnp.bfloat16),
        )
        right = jnp.where(
            bin_range[None, None, :] >= threshold_part[:, :, None],
            ratio_part[:, None, :],
            jnp.zeros((), jnp.bfloat16),
        ).reshape(-1, bin_count)
        return (
            total + lax.dot_general(left, right, pick, preferred_element_type=jnp.float32),
            None,
        )

    total, _ = lax.scan(
        add_block,
        jnp.zeros((account_count, bin_count), jnp.float32),
        jnp.arange(slot_count // block, dtype=jnp.int32),
    )
    whole = lax.psum(total, "terrain")
    net_whole = jnp.minimum(jnp.maximum(whole * scale - deductible[:, None], 0.0), limit[:, None])
    net_loss = net_whole.astype(jnp.bfloat16)[None]
    net_share = lax.dynamic_slice_in_dim(net_whole, lower, share_rows, 0)
    portfolio = lax.psum(net_share, "event") / (groups * lax.axis_size("event"))
    return (level, net_loss, portfolio)


def solution(mesh):
    placed = (
        P("event", "terrain", None),
        P("terrain", None),
        P("event", "terrain", None),
        P("terrain", None),
        P(),
        P(),
        P("terrain", None),
        P("terrain", None),
        P("terrain", None),
        P(),
        P(),
    )
    return jax.shard_map(
        per_device,
        mesh=mesh,
        in_specs=placed,
        out_specs=(P("event", "terrain", None), P("event", None, None), P("terrain", None)),
        check_vma=False,
    )
```

profile of v0, /device:TPU:0, one launch (start us, length us, event | category | flops | bytes accessed | tf_op | source)
XLA Modules:
  0.0 240.6 jit_solution(13161614519495146786)
XLA Ops:
  8.0 1.3 collective-permute-start.1
  9.3 3.0 %collective-permute-start = (f32[4,1,8,1024]{3,2,1,0:T(8,128)S(1)}, f32[4,1,8,1024]{3,2,1,0:T(8,128)S(1)}, u32[]{:S(2)}, u32[]{:S(2)}) collective-permute-start(f32[4,1,8,1024]{3,2,1,0:T(8,128)S(1)} %get-tuple-element.117), channel_id=1, source_target_pairs={{0,1},{1,2},{2,3},{3,4},{4,5},{5,6},{6,7},{8,9},{9,10},{10,11},{11... | collective-permute-start | bytes 393224 | tf_op jit(solution)/shard_map/ppermute | solution.py:21
  13.2 4.5 %collective-permute-start.2 = (s32[1,8,1024]{2,1,0:T(8,128)S(1)}, s32[1,8,1024]{2,1,0:T(8,128)S(1)}, u32[]{:S(2)}, u32[]{:S(2)}) collective-permute-start(s32[1,8,1024]{2,1,0:T(8,128)S(1)} %get-tuple-element.152), channel_id=1, source_target_pairs={{0,1},{1,2},{2,3},{3,4},{4,5},{5,6},{6,7},{8,9},{9,10},{10,11},{11... | collective-permute-start | bytes 98312 | tf_op jit(solution)/shard_map/ppermute | solution.py:21
  17.7 1.3 collective-permute-start.3
  22.7 5.3 %all-to-all-start.1 = ((bf16[8,1,48]{2,1,0:T(2,128)(2,1)}), bf16[8,1,48]{2,1,0:T(2,128)(2,1)S(1)}, u32[]{:S(2)}, u32[]{:S(2)}) async-start(bf16[8,1,48]{2,1,0:T(2,128)(2,1)} %convert_element_type.186), calls=%async_computation.1 | async-start | bytes 8192 | tf_op jit(solution)/shard_map/all_to_all | solution.py:117
  37.3 4.2 %all-to-all-start = ((bf16[8,48,256]{2,1,0:T(8,128)(2,1)}), bf16[8,48,256]{2,1,0:T(8,128)(2,1)S(1)}, u32[]{:S(2)}, u32[]{:S(2)}) async-start(bf16[8,48,256]{2,1,0:T(8,128)(2,1)} %bitcast.19), calls=%async_computation | async-start | bytes 393216 | tf_op jit(solution)/shard_map/all_to_all | solution.py:116
  41.7 6.0 %all-to-all-done = bf16[8,48,256]{2,1,0:T(8,128)(2,1)S(1)} async-done(((bf16[8,48,256]{2,1,0:T(8,128)(2,1)}), bf16[8,48,256]{2,1,0:T(8,128)(2,1)S(1)}, u32[]{:S(2)}, u32[]{:S(2)}) %all-to-all-start) | async-done | bytes 196640 | tf_op jit(solution)/shard_map/all_to_all | solution.py:116
  47.9 90.0 %while.11 = (s32[]{:T(128)}, f32[1024,256]{1,0:T(8,128)S(1)}, s32[12]{0:T(128)S(1)}, s32[384,128]{1,0:T(8,128)}, bf16[384,128]{1,0:T(8,128)(2,1)}, /*index=5*/s3...) while((s32[]{:T(128)}, f32[1024,256]{1,0:T(8,128)S(1)}, ...), condition=%wide.region_5.6_spmd.clone, body=%wide.region_4.5_spmd.clone.sunk | while | flops 2158493696 | bytes 6463685 | solution.py:148
  50.8 4.6 %fusion.203 = f32[1024,256]{1,0:T(8,128)S(1)} fusion(bf16[4096,256]{1,0:T(8,128)(2,1)S(1)} %bitcast.77, s32[4096]{0:T(1024)S(1)} %get-tuple-element.201, s32[4096]{0:T(1024)S(1)} %get-tuple-element.202, bf16[4096]{0:T(1024)(128)(2,1)S(1)} %dynamic-slice_bitcast_fusion.6, f32[1024,256]{1,0:T(8,128)S(1)} %get-tuple-element.215, pred[]{:T(512)S(6)} %compare.53), kind=kOutput, calls=%fused_computation.11.clone.1 | convolution fusion | flops 2158493696 | bytes 4235265 | tf_op jit(solution)/shard_map/while/body/eval_jaxpr/dot_general | solution.py:144
  58.3 4.6 %fusion.203 = f32[1024,256]{1,0:T(8,128)S(1)} fusion(bf16[4096,256]{1,0:T(8,128)(2,1)S(1)} %bitcast.77, s32[4096]{0:T(1024)S(1)} %get-tuple-element.201, s32[4096]{0:T(1024)S(1)} %get-tuple-element.202, bf16[4096]{0:T(1024)(128)(2,1)S(1)} %dynamic-slice_bitcast_fusion.6, f32[1024,256]{1,0:T(8,128)S(1)} %get-tuple-element.215, pred[]{:T(512)S(6)} %compare.53), kind=kOutput, calls=%fused_computation.11.clone.1 | convolution fusion | flops 2158493696 | bytes 4235265 | tf_op jit(solution)/shard_map/while/body/eval_jaxpr/dot_general | solution.py:144
  65.8 4.6 %fusion.203 = f32[1024,256]{1,0:T(8,128)S(1)} fusion(bf16[4096,256]{1,0:T(8,128)(2,1)S(1)} %bitcast.77, s32[4096]{0:T(1024)S(1)} %get-tuple-element.201, s32[4096]{0:T(1024)S(1)} %get-tuple-element.202, bf16[4096]{0:T(1024)(128)(2,1)S(1)} %dynamic-slice_bitcast_fusion.6, f32[1024,256]{1,0:T(8,128)S(1)} %get-tuple-element.215, pred[]{:T(512)S(6)} %compare.53), kind=kOutput, calls=%fused_computation.11.clone.1 | convolution fusion | flops 2158493696 | bytes 4235265 | tf_op jit(solution)/shard_map/while/body/eval_jaxpr/dot_general | solution.py:144
  73.3 4.6 %fusion.203 = f32[1024,256]{1,0:T(8,128)S(1)} fusion(bf16[4096,256]{1,0:T(8,128)(2,1)S(1)} %bitcast.77, s32[4096]{0:T(1024)S(1)} %get-tuple-element.201, s32[4096]{0:T(1024)S(1)} %get-tuple-element.202, bf16[4096]{0:T(1024)(128)(2,1)S(1)} %dynamic-slice_bitcast_fusion.6, f32[1024,256]{1,0:T(8,128)S(1)} %get-tuple-element.215, pred[]{:T(512)S(6)} %compare.53), kind=kOutput, calls=%fused_computation.11.clone.1 | convolution fusion | flops 2158493696 | bytes 4235265 | tf_op jit(solution)/shard_map/while/body/eval_jaxpr/dot_general | solution.py:144
  80.8 4.6 %fusion.203 = f32[1024,256]{1,0:T(8,128)S(1)} fusion(bf16[4096,256]{1,0:T(8,128)(2,1)S(1)} %bitcast.77, s32[4096]{0:T(1024)S(1)} %get-tuple-element.201, s32[4096]{0:T(1024)S(1)} %get-tuple-element.202, bf16[4096]{0:T(1024)(128)(2,1)S(1)} %dynamic-slice_bitcast_fusion.6, f32[1024,256]{1,0:T(8,128)S(1)} %get-tuple-element.215, pred[]{:T(512)S(6)} %compare.53), kind=kOutput, calls=%fused_computation.11.clone.1 | convolution fusion | flops 2158493696 | bytes 4235265 | tf_op jit(solution)/shard_map/while/body/eval_jaxpr/dot_general | solution.py:144
  88.3 4.6 %fusion.203 = f32[1024,256]{1,0:T(8,128)S(1)} fusion(bf16[4096,256]{1,0:T(8,128)(2,1)S(1)} %bitcast.77, s32[4096]{0:T(1024)S(1)} %get-tuple-element.201, s32[4096]{0:T(1024)S(1)} %get-tuple-element.202, bf16[4096]{0:T(1024)(128)(2,1)S(1)} %dynamic-slice_bitcast_fusion.6, f32[1024,256]{1,0:T(8,128)S(1)} %get-tuple-element.215, pred[]{:T(512)S(6)} %compare.53), kind=kOutput, calls=%fused_computation.11.clone.1 | convolution fusion | flops 2158493696 | bytes 4235265 | tf_op jit(solution)/shard_map/while/body/eval_jaxpr/dot_general | solution.py:144
  95.8 4.6 %fusion.203 = f32[1024,256]{1,0:T(8,128)S(1)} fusion(bf16[4096,256]{1,0:T(8,128)(2,1)S(1)} %bitcast.77, s32[4096]{0:T(1024)S(1)} %get-tuple-element.201, s32[4096]{0:T(1024)S(1)} %get-tuple-element.202, bf16[4096]{0:T(1024)(128)(2,1)S(1)} %dynamic-slice_bitcast_fusion.6, f32[1024,256]{1,0:T(8,128)S(1)} %get-tuple-element.215, pred[]{:T(512)S(6)} %compare.53), kind=kOutput, calls=%fused_computation.11.clone.1 | convolution fusion | flops 2158493696 | bytes 4235265 | tf_op jit(solution)/shard_map/while/body/eval_jaxpr/dot_general | solution.py:144
  103.3 4.6 %fusion.203 = f32[1024,256]{1,0:T(8,128)S(1)} fusion(bf16[4096,256]{1,0:T(8,128)(2,1)S(1)} %bitcast.77, s32[4096]{0:T(1024)S(1)} %get-tuple-element.201, s32[4096]{0:T(1024)S(1)} %get-tuple-element.202, bf16[4096]{0:T(1024)(128)(2,1)S(1)} %dynamic-slice_bitcast_fusion.6, f32[1024,256]{1,0:T(8,128)S(1)} %get-tuple-element.215, pred[]{:T(512)S(6)} %compare.53), kind=kOutput, calls=%fused_computation.11.clone.1 | convolution fusion | flops 2158493696 | bytes 4235265 | tf_op jit(solution)/shard_map/while/body/eval_jaxpr/dot_general | solution.py:144
  110.8 4.6 %fusion.203 = f32[1024,256]{1,0:T(8,128)S(1)} fusion(bf16[4096,256]{1,0:T(8,128)(2,1)S(1)} %bitcast.77, s32[4096]{0:T(1024)S(1)} %get-tuple-element.201, s32[4096]{0:T(1024)S(1)} %get-tuple-element.202, bf16[4096]{0:T(1024)(128)(2,1)S(1)} %dynamic-slice_bitcast_fusion.6, f32[1024,256]{1,0:T(8,128)S(1)} %get-tuple-element.215, pred[]{:T(512)S(6)} %compare.53), kind=kOutput, calls=%fused_computation.11.clone.1 | convolution fusion | flops 2158493696 | bytes 4235265 | tf_op jit(solution)/shard_map/while/body/eval_jaxpr/dot_general | solution.py:144
  118.3 4.6 %fusion.203 = f32[1024,256]{1,0:T(8,128)S(1)} fusion(bf16[4096,256]{1,0:T(8,128)(2,1)S(1)} %bitcast.77, s32[4096]{0:T(1024)S(1)} %get-tuple-element.201, s32[4096]{0:T(1024)S(1)} %get-tuple-element.202, bf16[4096]{0:T(1024)(128)(2,1)S(1)} %dynamic-slice_bitcast_fusion.6, f32[1024,256]{1,0:T(8,128)S(1)} %get-tuple-element.215, pred[]{:T(512)S(6)} %compare.53), kind=kOutput, calls=%fused_computation.11.clone.1 | convolution fusion | flops 2158493696 | bytes 4235265 | tf_op jit(solution)/shard_map/while/body/eval_jaxpr/dot_general | solution.py:144
  125.8 4.6 %fusion.203 = f32[1024,256]{1,0:T(8,128)S(1)} fusion(bf16[4096,256]{1,0:T(8,128)(2,1)S(1)} %bitcast.77, s32[4096]{0:T(1024)S(1)} %get-tuple-element.201, s32[4096]{0:T(1024)S(1)} %get-tuple-element.202, bf16[4096]{0:T(1024)(128)(2,1)S(1)} %dynamic-slice_bitcast_fusion.6, f32[1024,256]{1,0:T(8,128)S(1)} %get-tuple-element.215, pred[]{:T(512)S(6)} %compare.53), kind=kOutput, calls=%fused_computation.11.clone.1 | convolution fusion | flops 2158493696 | bytes 4235265 | tf_op jit(solution)/shard_map/while/body/eval_jaxpr/dot_general | solution.py:144
  133.3 4.6 %fusion.203 = f32[1024,256]{1,0:T(8,128)S(1)} fusion(bf16[4096,256]{1,0:T(8,128)(2,1)S(1)} %bitcast.77, s32[4096]{0:T(1024)S(1)} %get-tuple-element.201, s32[4096]{0:T(1024)S(1)} %get-tuple-element.202, bf16[4096]{0:T(1024)(128)(2,1)S(1)} %dynamic-slice_bitcast_fusion.6, f32[1024,256]{1,0:T(8,128)S(1)} %get-tuple-element.215, pred[]{:T(512)S(6)} %compare.53), kind=kOutput, calls=%fused_computation.11.clone.1 | convolution fusion | flops 2158493696 | bytes 4235265 | tf_op jit(solution)/shard_map/while/body/eval_jaxpr/dot_general | solution.py:144
  139.0 56.2 %all-reduce.33.cloned.1.call-done = f32[1024,256]{1,0:T(8,128)} async-done(((f32[1024,256]{1,0:T(8,128)}), f32[1024,256]{1,0:T(8,128)}) %all-reduce.33.cloned.1.call-update) | async-done | bytes 1048592 | tf_op jit(solution)/shard_map/psum | solution.py:153
  195.2 2.4 convert_bitcast_fusion
  198.2 34.0 %all-reduce.35.cloned.1.call-done = f32[128,256]{1,0:T(8,128)} async-done(((f32[128,256]{1,0:T(8,128)}), f32[128,256]{1,0:T(8,128)}) %all-reduce.35.cloned.1.call-update) | async-done | bytes 131088 | tf_op jit(solution)/shard_map/psum | solution.py:157
  232.2 1.6 broadcast_multiply_fusion
  (152 shorter events, 42.4 us)
Async XLA Ops:
  7.2 29.1 %copy-start = (bf16[128,256]{1,0:T(8,128)(2,1)S(1)}, bf16[128,256]{1,0:T(8,128)(2,1)}, u32[]{:S(2)}) copy-start(bf16[128,256]{1,0:T(8,128)(2,1)} %param.17) | copy-start | bytes 196612
  8.0 21.1 %collective-permute-start.1 = (f32[4,1,8,1024]{3,2,1,0:T(8,128)S(1)}, f32[4,1,8,1024]{3,2,1,0:T(8,128)S(1)}, u32[]{:S(2)}, u32[]{:S(2)}) collective-permute-start(f32[4,1,8,1024]{3,2,1,0:T(8,128)S(1)} %get-tuple-element.118), channel_id=1, source_target_pairs={{1,0},{2,1},{3,2},{4,3},{5,4},{6,5},{7,6},{9,8},{10,9},{11,10},{12... | collective-permute-start | bytes 393224 | tf_op jit(solution)/shard_map/ppermute | solution.py:23
  9.3 19.8 %collective-permute-start = (f32[4,1,8,1024]{3,2,1,0:T(8,128)S(1)}, f32[4,1,8,1024]{3,2,1,0:T(8,128)S(1)}, u32[]{:S(2)}, u32[]{:S(2)}) collective-permute-start(f32[4,1,8,1024]{3,2,1,0:T(8,128)S(1)} %get-tuple-element.117), channel_id=1, source_target_pairs={{0,1},{1,2},{2,3},{3,4},{4,5},{5,6},{6,7},{8,9},{9,10},{10,11},{11... | collective-permute-start | bytes 393224 | tf_op jit(solution)/shard_map/ppermute | solution.py:21
  13.2 15.0 %collective-permute-start.2 = (s32[1,8,1024]{2,1,0:T(8,128)S(1)}, s32[1,8,1024]{2,1,0:T(8,128)S(1)}, u32[]{:S(2)}, u32[]{:S(2)}) collective-permute-start(s32[1,8,1024]{2,1,0:T(8,128)S(1)} %get-tuple-element.152), channel_id=1, source_target_pairs={{0,1},{1,2},{2,3},{3,4},{4,5},{5,6},{6,7},{8,9},{9,10},{10,11},{11... | collective-permute-start | bytes 98312 | tf_op jit(solution)/shard_map/ppermute | solution.py:21
  17.7 11.5 %collective-permute-start.3 = (s32[1,8,1024]{2,1,0:T(8,128)S(1)}, s32[1,8,1024]{2,1,0:T(8,128)S(1)}, u32[]{:S(2)}, u32[]{:S(2)}) collective-permute-start(s32[1,8,1024]{2,1,0:T(8,128)S(1)} %get-tuple-element.151), channel_id=1, source_target_pairs={{1,0},{2,1},{3,2},{4,3},{5,4},{6,5},{7,6},{9,8},{10,9},{11,10},{12... | collective-permute-start | bytes 98312 | tf_op jit(solution)/shard_map/ppermute | solution.py:23
  22.7 14.6 %all-to-all-start.1 = ((bf16[8,1,48]{2,1,0:T(2,128)(2,1)}), bf16[8,1,48]{2,1,0:T(2,128)(2,1)S(1)}, u32[]{:S(2)}, u32[]{:S(2)}) async-start(bf16[8,1,48]{2,1,0:T(2,128)(2,1)} %convert_element_type.186), calls=%async_computation.1 | async-start | bytes 8192 | tf_op jit(solution)/shard_map/all_to_all | solution.py:117
  34.7 1.5 copy-start.4
  37.3 10.4 %all-to-all-start = ((bf16[8,48,256]{2,1,0:T(8,128)(2,1)}), bf16[8,48,256]{2,1,0:T(8,128)(2,1)S(1)}, u32[]{:S(2)}, u32[]{:S(2)}) async-start(bf16[8,48,256]{2,1,0:T(8,128)(2,1)} %bitcast.19), calls=%async_computation | async-start | bytes 393216 | tf_op jit(solution)/shard_map/all_to_all | solution.py:116
  41.5 153.6 %all-reduce.33.cloned.1.call-start = ((), (), s32[]{:S(2)}) async-start(), calls=%async_computation.2 | async-start | bytes 2097152 | tf_op jit(solution)/shard_map/psum | solution.py:153
  47.9 147.3 %copy-start.2 = (f32[1024]{0:T(1024)S(1)}, f32[1024]{0:T(1024)}, u32[]{:S(2)}) copy-start(f32[1024]{0:T(1024)} %param.23) | copy-start | bytes 12292
  47.9 147.3 %copy-start.3 = (f32[1024]{0:T(1024)S(1)}, f32[1024]{0:T(1024)}, u32[]{:S(2)}) copy-start(f32[1024]{0:T(1024)} %param.22) | copy-start | bytes 12292
  137.9 1.0 copy-start.1
  139.0 93.3 %all-reduce.35.cloned.1.call-start = ((), (), s32[]{:S(2)}) async-start(), calls=%async_computation.3 | async-start | bytes 262144 | tf_op jit(solution)/shard_map/psum | solution.py:157
Sparse Core Ops, SparseCore 0:
  139.1 56.0 all-reduce.32
  198.3 33.8 all-reduce.34
where the time goes:
time: 244 us; the launch traced here: 241 us
  waiting for transfers between devices  96.3 us (39%)
  matrix products  56.6 us (23%)
  local copies, waits for them, and re-layouts  31.2 us (13%)
  starting transfers between devices  19.7 us (8%)
  between operations  14.6 us (6%)
  other arithmetic  14 us (6%)
  loops' own time  8.35 us (3%)
    psum x1, waiting for transfers between devices, per_device(): whole = lax.psum(total, 'terrain')  56.2 us
    dot_general x12, matrix products, add_block(): lax.dot_general(left, right, pick, preferred_element_type=jnp.float32)  55.5 us
    psum x1, waiting for transfers between devices, per_device(): portfolio = lax.psum(net_share, 'event') / (groups * lax.axis_size('event'))  34 us
    ge x12, local copies, waits for them, and re-layouts, add_block(): bin_range[None, None, :] >= threshold_part[:, :, None]  8.95 us
    broadcast_in_dim x12, local copies, waits for them, and re-layouts, add_block(): jnp.where(account_part[:, None] == columns[None, :], value_part[:, None],...  8.37 us
    another operation x1, loops' own time, per_device(): lax.scan(add_block, jnp.zeros((account_count, bin_count), jnp.float32), j...  8.35 us
    ppermute x2, starting transfers between devices, with_halo(): lax.ppermute(tail, axis, [(i, (i + 1) % count) for i in range(ends)])  7.51 us
    dynamic_slice x12, local copies, waits for them, and re-layouts, per_device(): lax.scan(add_block, jnp.zeros((account_count, bin_count), jnp.float32), j...  7.04 us
  transfers between devices with their start and end apart: 8, of which 3 were waited for; matrix products, arithmetic and copies ran while one was open for 6% of the time, Pallas kernels for 0%

commit v1 on v0

v1 whole, which is shorter than its diff:
```python
import functools

import jax
import jax.numpy as jnp
from jax import lax
from jax.experimental import pallas as pl
from jax.experimental.pallas import tpu as pltpu
from jax.sharding import PartitionSpec as P

SUBSTEPS = 8
CHUNK = 8
LOW = 256

courant = 0.5
gravity = 1.0

VMEM = pl.BlockSpec(memory_space=pltpu.VMEM)
SMEM = pl.BlockSpec(memory_space=pltpu.SMEM)
MESH = pl.DeviceIdType.MESH


def exchange_kernel(jobs, *refs):
    count = len(jobs)
    sources, targets, sems = refs[:count], refs[count : 2 * count], refs[2 * count :]
    barrier = pltpu.get_barrier_semaphore()
    greeted = 0
    for axis in dict.fromkeys(axis for axis, _ in jobs):
        size = lax.axis_size(axis)
        me = lax.axis_index(axis)
        for hop in range(1, size):
            pl.semaphore_signal(
                barrier, inc=1, device_id={axis: lax.rem(me + hop, size)}, device_id_type=MESH
            )
        greeted += size - 1
    pl.semaphore_wait(barrier, greeted)
    copies = []
    for job, (axis, spread) in enumerate(jobs):
        source, target = sources[job], targets[job]
        local, sent, received = sems[3 * job : 3 * job + 3]
        size = lax.axis_size(axis)
        me = lax.axis_index(axis)
        for hop in range(1, size):
            peer = lax.rem(me + hop, size)
            copy = pltpu.make_async_remote_copy(
                src_ref=source if spread else source.at[peer],
                dst_ref=target.at[me],
                send_sem=sent.at[hop],
                recv_sem=received.at[hop],
                device_id={axis: peer},
                device_id_type=MESH,
            )
            copy.start()
            copies.append(copy)
        own = pltpu.make_async_copy(source if spread else source.at[me], target.at[me], local)
        own.start()
        copies.append(own)
    for copy in copies:
        copy.wait()


def exchange(arrays, jobs, number):
    shapes, scratch = [], []
    for array, (axis, spread) in zip(arrays, jobs):
        size = lax.axis_size(axis)
        shape = (size,) + array.shape if spread else array.shape
        shapes.append(jax.ShapeDtypeStruct(shape, array.dtype))
        scratch += [
            pltpu.SemaphoreType.DMA,
            pltpu.SemaphoreType.DMA((size,)),
            pltpu.SemaphoreType.DMA((size,)),
        ]
    return pl.pallas_call(
        functools.partial(exchange_kernel, jobs),
        out_shape=shapes,
        in_specs=[VMEM] * len(arrays),
        out_specs=[VMEM] * len(arrays),
        scratch_shapes=scratch,
        compiler_params=pltpu.CompilerParams(collective_id=number, has_side_effects=True),
        name="exchange" + str(number),
    )(*arrays)


def flood_kernel(
    rows, slot_count, capacity, above, here, below, wet_above, wet_here, wet_below,
    owner_row, owner_column, weight, bias, level_out, outgoing_out,
):
    first_row = lax.axis_index("terrain") * rows - SUBSTEPS
    total_rows = rows * lax.axis_size("terrain")
    level = jnp.concatenate([above[0], here[0], below[0]], axis=0)
    bed = jnp.concatenate([above[1], here[1], below[1]], axis=0)
    wet = jnp.concatenate([wet_above[...], wet_here[...], wet_below[...]], axis=0)
    shape = level.shape
    tall, width = shape
    row_id = first_row + lax.broadcasted_iota(jnp.int32, shape, 0)
    column = lax.broadcasted_iota(jnp.int32, shape, 1)
    inside = ((row_id >= 0) & (row_id < total_rows)).astype(jnp.float32)
    not_first = (column > 0).astype(jnp.float32)
    not_last = (column < width - 1).astype(jnp.float32)

    def down(field):
        return pltpu.roll(field, tall - 1, 0)

    def up(field):
        return pltpu.roll(field, 1, 0)

    def right(field):
        return pltpu.roll(field, width - 1, 1) * not_last

    def left(field):
        return pltpu.roll(field, 1, 1) * not_first

    row_speed = jnp.zeros(shape, jnp.float32)
    col_speed = jnp.zeros(shape, jnp.float32)
    for step in range(SUBSTEPS):
        wet_factor = ((wet >> step) & 1).astype(jnp.float32) * inside
        ld, lu, lr, ll = down(level), up(level), right(level), left(level)
        new_level = 0.25 * (ld + lu + lr + ll)
        if step:
            row_flow, col_flow = bed * row_speed, bed * col_speed
            new_level = new_level - 0.5 * courant * (
                down(row_flow) - up(row_flow) + (right(col_flow) - left(col_flow))
            )
            row_mean = 0.25 * (
                down(row_speed) + up(row_speed) + right(row_speed) + left(row_speed)
            )
            col_mean = 0.25 * (
                down(col_speed) + up(col_speed) + right(col_speed) + left(col_speed)
            )
            row_speed = (row_mean - 0.5 * courant * gravity * (ld - lu)) * wet_factor
            col_speed = (col_mean - 0.5 * courant * gravity * (lr - ll)) * wet_factor
        else:
            row_speed = (0.0 - 0.5 * courant * gravity * (ld - lu)) * wet_factor
            col_speed = (0.0 - 0.5 * courant * gravity * (lr - ll)) * wet_factor
        level = new_level * inside
    level = level[SUBSTEPS : SUBSTEPS + rows]
    level_out[...] = level
    tile = weight.shape[0]
    blocks = width // tile
    pieces = jnp.concatenate(
        [level[:, j * tile : (j + 1) * tile] for j in range(blocks)], axis=0
    ).astype(jnp.bfloat16)
    ratio = jax.nn.sigmoid(
        jnp.dot(pieces, weight[...], preferred_element_type=jnp.float32) + bias[...]
    ).astype(jnp.bfloat16)
    tiles = rows * blocks
    along = lax.broadcasted_iota(jnp.int32, (tiles, tiles), 1)
    across = lax.broadcasted_iota(jnp.int32, (tiles, tiles), 0)

    def number(place):
        return (place % rows) * blocks + place // rows

    earlier = (owner_column[...] == owner_row[...]) & (number(across) < number(along))
    rank = jnp.sum(earlier.astype(jnp.float32), axis=0, keepdims=True).astype(jnp.int32)
    place = owner_row[...] * capacity + rank
    slot = lax.broadcasted_iota(jnp.int32, (slot_count, tiles), 0)
    chosen = jnp.where(slot == place, 1.0, 0.0).astype(jnp.bfloat16)
    outgoing_out[...] = jnp.dot(chosen, ratio, preferred_element_type=jnp.float32).astype(
        jnp.bfloat16
    )


def loss_kernel(busy, ratio, account, threshold, value, total, left, right):
    accounts, bins = total.shape
    slots, tile = account.shape
    high_count = accounts // LOW
    total[...] = jnp.zeros(total.shape, jnp.float32)
    sub = 16
    low_id = (
        lax.broadcasted_iota(jnp.int32, (LOW, tile), 0).astype(jnp.float32).astype(jnp.bfloat16)
    )
    bin_id = (
        lax.broadcasted_iota(jnp.int32, (sub, bins), 1).astype(jnp.float32).astype(jnp.bfloat16)
    )
    bin_id = jnp.concatenate([bin_id] * (tile // sub), axis=0)

    def rowed(row, height):
        packed = jnp.broadcast_to(row, (sub, row.shape[1])).astype(jnp.bfloat16)
        return jnp.concatenate([packed] * (height // sub), axis=0)

    def chunk(number, _):
        @pl.when(busy[number] != 0)
        def _():
            first = pl.multiple_of(number * CHUNK, CHUNK)
            accounts_now = account[pl.ds(first, CHUNK), :]
            low = (accounts_now & (LOW - 1)).astype(jnp.float32)
            high = accounts_now // LOW
            values = value[pl.ds(first, CHUNK), :]
            bounds = jnp.transpose(threshold[pl.ds(first, CHUNK), :].astype(jnp.float32))
            ratios = ratio[pl.ds(first, CHUNK), :]
            parts = [jnp.where(high == h, values, 0.0) for h in range(high_count)]
            for i in range(CHUNK):
                cells = slice(i * tile, (i + 1) * tile)
                hit = rowed(low[i : i + 1], LOW) == low_id
                for h in range(high_count):
                    left[h * LOW : (h + 1) * LOW, cells] = jnp.where(
                        hit, rowed(parts[h][i : i + 1], LOW), jnp.zeros((), jnp.bfloat16)
                    )
                bound = jnp.broadcast_to(bounds[:, i : i + 1], (tile, bins)).astype(jnp.bfloat16)
                right[cells, :] = jnp.where(
                    bin_id >= bound, rowed(ratios[i : i + 1], tile), jnp.zeros((), jnp.bfloat16)
                )
            total[...] += jnp.dot(left[...], right[...], preferred_element_type=jnp.float32)

        return 0

    lax.fori_loop(0, slots // CHUNK, chunk, 0)


def per_device(
    level_start,
    bed_depth,
    wet_bits,
    tile_owner,
    vuln_weight,
    vuln_bias,
    account_index,
    bin_index,
    exposure_value,
    deductible,
    limit,
):
    _, rows, width = level_start.shape
    tile_cells, bin_count = vuln_weight.shape
    account_count = deductible.shape[0]
    owners = lax.axis_size("terrain")
    events = lax.axis_size("event")
    slot_count = account_index.shape[0]
    capacity = slot_count // owners
    share_rows = account_count // owners
    blocks = width // tile_cells
    tiles = rows * blocks

    here = jnp.stack([level_start[0], bed_depth])
    wet = wet_bits[0]
    forth = [(i, i + 1) for i in range(owners - 1)]
    back = [(i + 1, i) for i in range(owners - 1)]
    above = lax.ppermute(here[:, rows - SUBSTEPS :], "terrain", forth)
    below = lax.ppermute(here[:, :SUBSTEPS], "terrain", back)
    wet_above = lax.ppermute(wet[rows - SUBSTEPS :], "terrain", forth)
    wet_below = lax.ppermute(wet[:SUBSTEPS], "terrain", back)
    owner = tile_owner[:, 0].reshape(rows, blocks).T.reshape(1, tiles)
    level, outgoing = pl.pallas_call(
        functools.partial(flood_kernel, rows, slot_count, capacity),
        out_shape=(
            jax.ShapeDtypeStruct((rows, width), jnp.float32),
            jax.ShapeDtypeStruct((slot_count, bin_count), jnp.bfloat16),
        ),
        in_specs=[VMEM] * 10,
        out_specs=(VMEM, VMEM),
        name="flood",
    )(
        above, here, below, wet_above, wet, wet_below,
        owner, owner.reshape(tiles, 1), vuln_weight, vuln_bias[None, :],
    )
    outgoing = outgoing.reshape(owners, capacity, bin_count)
    (ratio,) = exchange([outgoing], [("terrain", False)], 1)
    ratio = ratio.reshape(slot_count, bin_count).astype(jnp.float32)
    busy = jnp.any(ratio.reshape(slot_count // CHUNK, -1) != 0, axis=1).astype(jnp.int32)
    total = pl.pallas_call(
        loss_kernel,
        out_shape=jax.ShapeDtypeStruct((account_count, bin_count), jnp.float32),
        in_specs=[SMEM] + [VMEM] * 4,
        out_specs=VMEM,
        scratch_shapes=[
            pltpu.VMEM((account_count, CHUNK * tile_cells), jnp.bfloat16),
            pltpu.VMEM((CHUNK * tile_cells, bin_count), jnp.bfloat16),
        ],
        name="losses",
    )(busy, ratio, account_index, bin_index, exposure_value.astype(jnp.float32))
    (parts,) = exchange(
        [total.reshape(owners, share_rows, bin_count)], [("terrain", False)], 2
    )
    scale = account_count / (rows * width * owners)
    lower = lax.axis_index("terrain") * share_rows
    floor = lax.dynamic_slice_in_dim(deductible, lower, share_rows, 0)[:, None]
    roof = lax.dynamic_slice_in_dim(limit, lower, share_rows, 0)[:, None]
    whole = jnp.sum(parts, axis=0)
    net = jnp.minimum(jnp.maximum(whole * scale - floor, 0.0), roof)
    net_loss, nets = exchange(
        [net.astype(jnp.bfloat16), net], [("terrain", True), ("event", True)], 3
    )
    portfolio = jnp.sum(nets, axis=0) / events
    return (level[None], net_loss.reshape(1, account_count, bin_count), portfolio)


def solution(mesh):
    placed = (
        P("event", "terrain", None),
        P("terrain", None),
        P("event", "terrain", None),
        P("terrain", None),
        P(),
        P(),
        P("terrain", None),
        P("terrain", None),
        P("terrain", None),
        P(),
        P(),
    )
    return jax.shard_map(
        per_device,
        mesh=mesh,
        in_specs=placed,
        out_specs=(P("event", "terrain", None), P("event", None, None), P("terrain", None)),
        check_vma=False,
    )
```

time: 244 us -> 122 us (0.50); the launches traced: 241 us -> 122 us
  waiting for transfers between devices: 96.3 us -> 0.01 us
  Pallas kernels: 0 us -> 96.1 us
  matrix products: 56.6 us -> 0 us
  local copies, waits for them, and re-layouts: 31.2 us -> 5.18 us
  between operations: 14.6 us -> 0.84 us
  starting transfers between devices: 19.7 us -> 10.2 us
  loops' own time: 8.35 us -> 0 us
  other arithmetic: 14 us -> 9.45 us
    pallas_call x0 -> x5, Pallas kernels: none -> 96.1 us  [the longest x1 46.6 us: per_device(): pl.pallas_call(loss_kernel, out_shape=jax.ShapeDtypeStruct((account_count...]
    psum x2 -> x0, waiting for transfers between devices: 90.2 us -> none  [the longest x1 56.2 us: per_device(): whole = lax.psum(total, 'terrain')]
    dot_general x13 -> x0, matrix products: 56.6 us -> none  [the longest x12 55.5 us: add_block(): lax.dot_general(left, right, pick, preferred_element_type=jnp.float32)]
    broadcast_in_dim x31 -> x0, local copies, waits for them, and re-layouts: 10.2 us -> none  [the longest x12 8.37 us: add_block(): jnp.where(account_part[:, None] == columns[None, :], value_part[:, None],...]
    all_to_all x2 -> x0, starting transfers between devices: 9.52 us -> none  [the longest x1 5.33 us: per_device(): lax.all_to_all(marks_out, 'terrain', split_axis=0, concat_axis=0, tiled=T...]
    ge x12 -> x0, local copies, waits for them, and re-layouts: 8.95 us -> none  [add_block(): bin_range[None, None, :] >= threshold_part[:, :, None]]
    another operation x1 -> x0, loops' own time: 8.35 us -> none  [per_device(): lax.scan(add_block, jnp.zeros((account_count, bin_count), jnp.float32), j...]
    dynamic_slice x25 -> x2, local copies, waits for them, and re-layouts: 7.81 us -> 1.52 us  [the longest x1 0.76 us: per_device(): floor = lax.dynamic_slice_in_dim(deductible, lower, share_rows, 0)[:, None]]
  transfers between devices with their start and end apart: 8 -> 4, of which waited for: 3 -> 0; matrix products, arithmetic and copies ran while one was open for 6% -> 5% of each run, Pallas kernels for 0% -> 0%
where the time goes in v1:
time: 122 us
  Pallas kernels  96.1 us (79%)
  starting transfers between devices  10.2 us (8%)
  other arithmetic  9.45 us (8%)
  local copies, waits for them, and re-layouts  5.18 us (4%)
    pallas_call x1, Pallas kernels, per_device(): pl.pallas_call(loss_kernel, out_shape=jax.ShapeDtypeStruct((account_count...  46.6 us
    pallas_call x3, Pallas kernels, exchange(): pl.pallas_call(functools.partial(exchange_kernel, jobs), out_shape=shapes...  44.2 us
    pallas_call x1, Pallas kernels, per_device(): pl.pallas_call(functools.partial(flood_kernel, rows, slot_count, capacity...  5.36 us
    ppermute x1, starting transfers between devices, per_device(): wet_above = lax.ppermute(wet[rows - SUBSTEPS:], 'terrain', forth)  5.12 us
    ppermute x1, starting transfers between devices, per_device(): above = lax.ppermute(here[:, rows - SUBSTEPS:], 'terrain', forth)  2.53 us
  transfers between devices with their start and end apart: 4, of which 0 were waited for; matrix products, arithmetic and copies ran while one was open for 5% of the time, Pallas kernels for 0%

profile of v1, /device:TPU:0, one launch (start us, length us, event | category | flops | bytes accessed | tf_op | source)
XLA Modules:
  0.0 121.9 jit_solution(1615595433581661235)
XLA Ops:
  0.7 0.9 fusion.1
  1.5 2.5 %collective-permute-start = (f32[2,8,1024]{2,1,0:T(8,128)S(1)}, f32[2,8,1024]{2,1,0:T(8,128)S(1)}, u32[]{:S(2)}, u32[]{:S(2)}) collective-permute-start(f32[2,8,1024]{2,1,0:T(8,128)S(1)} %get-tuple-element.14), channel_id=1, source_target_pairs={{0,1},{1,2},{2,3},{3,4},{4,5},{5,6},{6,7},{8,9},{9,10},{10,11},{11... | collective-permute-start | bytes 196616 | tf_op jit(solution)/shard_map/ppermute | solution.py:237
  4.1 1.3 %collective-permute-start.1 = (f32[2,8,1024]{2,1,0:T(8,128)S(1)}, f32[2,8,1024]{2,1,0:T(8,128)S(1)}, u32[]{:S(2)}, u32[]{:S(2)}) collective-permute-start(f32[2,8,1024]{2,1,0:T(8,128)S(1)} %get-tuple-element.13), channel_id=1, source_target_pairs={{1,0},{2,1},{3,2},{4,3},{5,4},{6,5},{7,6},{9,8},{10,9},{11,10},{12... | collective-permute-start | bytes 196616 | tf_op jit(solution)/shard_map/ppermute | solution.py:238
  5.4 5.1 %collective-permute-start.2 = (s32[8,1024]{1,0:T(8,128)S(1)}, s32[8,1024]{1,0:T(8,128)S(1)}, u32[]{:S(2)}, u32[]{:S(2)}) collective-permute-start(s32[8,1024]{1,0:T(8,128)S(1)} %get-tuple-element.16), channel_id=1, source_target_pairs={{0,1},{1,2},{2,3},{3,4},{4,5},{5,6},{6,7},{8,9},{9,10},{10,11},{11... | collective-permute-start | bytes 98312 | tf_op jit(solution)/shard_map/ppermute | solution.py:239
  10.5 1.3 %collective-permute-start.3 = (s32[8,1024]{1,0:T(8,128)S(1)}, s32[8,1024]{1,0:T(8,128)S(1)}, u32[]{:S(2)}, u32[]{:S(2)}) collective-permute-start(s32[8,1024]{1,0:T(8,128)S(1)} %get-tuple-element.15), channel_id=1, source_target_pairs={{1,0},{2,1},{3,2},{4,3},{5,4},{6,5},{7,6},{9,8},{10,9},{11,10},{12... | collective-permute-start | bytes 98312 | tf_op jit(solution)/shard_map/ppermute | solution.py:240
  11.9 0.7 pad_maximum_fusion.here
  13.1 0.7 reduce.5
  13.9 0.8 reshape_reshape.4.owner_column
  14.7 0.6 reshape.28.owner_row
  15.4 0.7 convert_element_type.20.value
  16.1 0.8 dynamic_slice.6
  16.8 0.8 dynamic_slice.7
  17.6 0.5 copy-done.8
  18.3 5.4 %flood.1 = (f32[32,1024]{1,0:T(8,128)}, bf16[384,256]{1,0:T(8,128)(2,1)}) custom-call(f32[2,8,1024]{2,1,0:T(8,128)} %copy-done.6, f32[2,32,1024]{2,1,0:T(8,128)} %pad_maximum_fusion.here, f32[2,8,1024]{2,1,0:T(8,128)} %copy-done.7, s32[8,1024]{1,0:T(8,128)} %copy-done.8, s32[32,1024]{1,0:T(8,128)} %bitcast.20, s32[8,1024]{1,0:T(8,128)} %copy-done.9, ...), custom_call_target="tpu_custom_call" | custom-call | tf_op jit(solution)/shard_map/flood/pallas_call | solution.py:242
  23.6 11.8 %exchange1.1 = bf16[8,48,256]{2,1,0:T(8,128)(2,1)} custom-call(bf16[8,48,256]{2,1,0:T(8,128)(2,1)} %bitcast.21), custom_call_target="tpu_custom_call" | custom-call | tf_op jit(solution)/shard_map/exchange1/pallas_call | solution.py:72
  35.5 1.8 %bitcast_convert_fusion.ratio = f32[384,256]{1,0:T(8,128)} fusion(bf16[8,48,256]{2,1,0:T(8,128)(2,1)} %exchange1.1), kind=kLoop, calls=%fused_computation.13 | loop fusion | flops 98304 | bytes 589824 | tf_op jit(solution)/shard_map/convert_element_type | solution.py:257
  38.2 46.6 %losses.1 = f32[1024,256]{1,0:T(8,128)} custom-call(s32[48]{0:T(128)} %convert_element_type.17.busy, f32[384,256]{1,0:T(8,128)} %bitcast_convert_fusion.ratio, s32[384,128]{1,0:T(8,128)} %account.1, s32[384,128]{1,0:T(8,128)} %threshold.1, f32[384,128]{1,0:T(8,128)} %convert_element_type.20.value), custom_call_target="tpu_custom_call" | custom-call | tf_op jit(solution)/shard_map/losses/pallas_call | solution.py:259
  84.8 14.6 %exchange2.1 = f32[8,128,256]{2,1,0:T(8,128)} custom-call(f32[8,128,256]{2,1,0:T(8,128)} %bitcast.16), custom_call_target="tpu_custom_call" | custom-call | tf_op jit(solution)/shard_map/exchange2/pallas_call | solution.py:72
  99.4 1.3 %reduce_sum.18 = f32[128,256]{1,0:T(8,128)S(1)} reduce(f32[8,128,256]{2,1,0:T(8,128)} %exchange2.1, f32[]{:T(128)} %constant.8.clone.1), dimensions={0}, to_apply=%region_2.0 | reduce | flops 229376 | bytes 1179652 | tf_op jit(solution)/shard_map/reduce_sum | solution.py:277
  100.7 0.8 fusion.2
  101.5 17.8 %exchange3.1 = (bf16[8,128,256]{2,1,0:T(8,128)(2,1)}, f32[4,128,256]{2,1,0:T(8,128)}) custom-call(bf16[128,256]{1,0:T(8,128)(2,1)} %get-tuple-element.11.refs_0_, f32[128,256]{1,0:T(8,128)} %get-tuple-element.12.refs_1_), custom_call_target="tpu_custom_call" | custom-call | tf_op jit(solution)/shard_map/exchange3/pallas_call | solution.py:72
  119.3 1.1 reduce_sum.19
  120.4 0.7 broadcast_multiply_fusion
  121.1 0.8 copy.19
  (33 shorter events, 1.7 us)
Async XLA Ops:
  0.6 4.7 %copy-start.4 = (s32[1,32,1024]{2,1,0:T(8,128)S(1)}, s32[1,32,1024]{2,1,0:T(8,128)}, u32[]{:S(2)}) copy-start(s32[1,32,1024]{2,1,0:T(8,128)} %param.13) | copy-start | bytes 393220
  0.6 11.2 %copy-start.3 = (f32[32,1024]{1,0:T(8,128)S(1)}, f32[32,1024]{1,0:T(8,128)}, u32[]{:S(2)}) copy-start(f32[32,1024]{1,0:T(8,128)} %param.12) | copy-start | bytes 393220
  1.5 10.3 %copy-start.2 = (f32[1,32,1024]{2,1,0:T(8,128)S(1)}, f32[1,32,1024]{2,1,0:T(8,128)}, u32[]{:S(2)}) copy-start(f32[1,32,1024]{2,1,0:T(8,128)} %param.11) | copy-start | bytes 393220
  1.5 16.1 %collective-permute-start = (f32[2,8,1024]{2,1,0:T(8,128)S(1)}, f32[2,8,1024]{2,1,0:T(8,128)S(1)}, u32[]{:S(2)}, u32[]{:S(2)}) collective-permute-start(f32[2,8,1024]{2,1,0:T(8,128)S(1)} %get-tuple-element.14), channel_id=1, source_target_pairs={{0,1},{1,2},{2,3},{3,4},{4,5},{5,6},{6,7},{8,9},{9,10},{10,11},{11... | collective-permute-start | bytes 196616 | tf_op jit(solution)/shard_map/ppermute | solution.py:237
  4.1 13.6 %collective-permute-start.1 = (f32[2,8,1024]{2,1,0:T(8,128)S(1)}, f32[2,8,1024]{2,1,0:T(8,128)S(1)}, u32[]{:S(2)}, u32[]{:S(2)}) collective-permute-start(f32[2,8,1024]{2,1,0:T(8,128)S(1)} %get-tuple-element.13), channel_id=1, source_target_pairs={{1,0},{2,1},{3,2},{4,3},{5,4},{6,5},{7,6},{9,8},{10,9},{11,10},{12... | collective-permute-start | bytes 196616 | tf_op jit(solution)/shard_map/ppermute | solution.py:238
  5.4 12.2 %collective-permute-start.2 = (s32[8,1024]{1,0:T(8,128)S(1)}, s32[8,1024]{1,0:T(8,128)S(1)}, u32[]{:S(2)}, u32[]{:S(2)}) collective-permute-start(s32[8,1024]{1,0:T(8,128)S(1)} %get-tuple-element.16), channel_id=1, source_target_pairs={{0,1},{1,2},{2,3},{3,4},{4,5},{5,6},{6,7},{8,9},{9,10},{10,11},{11... | collective-permute-start | bytes 98312 | tf_op jit(solution)/shard_map/ppermute | solution.py:239
  10.5 7.1 %collective-permute-start.3 = (s32[8,1024]{1,0:T(8,128)S(1)}, s32[8,1024]{1,0:T(8,128)S(1)}, u32[]{:S(2)}, u32[]{:S(2)}) collective-permute-start(s32[8,1024]{1,0:T(8,128)S(1)} %get-tuple-element.15), channel_id=1, source_target_pairs={{1,0},{2,1},{3,2},{4,3},{5,4},{6,5},{7,6},{9,8},{10,9},{11,10},{12... | collective-permute-start | bytes 98312 | tf_op jit(solution)/shard_map/ppermute | solution.py:240
  11.8 1.2 %copy-start.10 = (s32[256,1]{0,1:T(1,128)S(1)}, s32[256,1]{0,1:T(1,128)}, u32[]{:S(2)}) copy-start(s32[256,1]{0,1:T(1,128)} %param.14) | copy-start | bytes 3076
  12.6 2.8 %copy-start.5 = (bf16[384,128]{1,0:T(8,128)(2,1)S(1)}, bf16[384,128]{1,0:T(8,128)(2,1)}, u32[]{:S(2)}) copy-start(bf16[384,128]{1,0:T(8,128)(2,1)} %param.19) | copy-start | bytes 294916
  17.6 0.6 copy-start.8
  17.6 0.6 copy-start.9
  17.6 0.6 copy-start.6
  17.6 0.6 copy-start.7
  35.5 1.8 %copy-start = (bf16[8,48,256]{2,1,0:T(8,128)(2,1)S(1)}, bf16[8,48,256]{2,1,0:T(8,128)(2,1)}, u32[]{:S(2)}) copy-start(bf16[8,48,256]{2,1,0:T(8,128)(2,1)} %exchange1.1) | copy-start | bytes 589828
  119.3 1.8 %copy-start.1 = (bf16[8,128,256]{2,1,0:T(8,128)(2,1)S(1)}, bf16[8,128,256]{2,1,0:T(8,128)(2,1)}, u32[]{:S(2)}) copy-start(bf16[8,128,256]{2,1,0:T(8,128)(2,1)} %get-tuple-element.9) | copy-start | bytes 1572868
